TPU v7x, 256 devices: a whole 4x4x8 slice. The times are simulated.
256 devices in a mesh: branch: 2 (over core), gi: 16 (over y_hi, z), gj: 8 (over x, y_lo).
Axes of the slice: x: 4, y: 4 (y_hi: 2, y_lo: 2; y = y_hi * 2 + y_lo), z: 8, core: 2. Of those that a mesh axis runs over, the one named last changes fastest.
Arguments:
- homolog_embedding: float32 [128, 256, 256], P(('branch', 'gj'), 'gi'), may hold values from -6 to 6
- pair_input_tensor: float32 [256, 256, 128], P('gi', ('branch', 'gj')), may hold values from -6 to 6
- layernorm_scales: float32 [4, 256], replicated, may hold values from 0.5 to 1.5
- pair_norm_gains: float32 [3, 128], replicated, may hold values from 0.5 to 1.5
- pair_bias_matrix: float32 [128, 8], replicated
- horizontal_qkvg_kernel: float32 [256, 1024], replicated, may hold values from -0.375 to 0.375
- horizontal_final_kernel: float32 [256, 256], replicated, may hold values from -0.375 to 0.375
- vertical_qkvg_kernel: float32 [256, 1024], replicated, may hold values from -0.375 to 0.375
- vertical_final_kernel: float32 [256, 256], replicated, may hold values from -0.375 to 0.375
- feedforward_expand_kernel: float32 [256, 1024], replicated, may hold values from -0.375 to 0.375
- feedforward_shrink_kernel: float32 [1024, 256], replicated, may hold values from -0.1875 to 0.1875
- dyadic_sides_kernel: float32 [256, 64], replicated, may hold values from -0.375 to 0.375
- outer_output_matrix: float32 [1024, 128], replicated, may hold values from -1 to 1
- triangle_input_matrix: float32 [128, 640], replicated, may hold values from -0.5 to 0.5
- triangle_output_matrix: float32 [128, 128], replicated, may hold values from -0.5 to 0.5
Outputs:
- alignment_output: float32 [128, 256, 256], P(('branch', 'gj'), 'gi')
- pair_output_tensor: float32 [256, 256, 128], P('gi', ('branch', 'gj'))
All inputs are finite; a program needn't handle non-finite values.
Results may differ from a plain program's by a relative error of at most 0.0003.
Values sent between devices are 32-bit elements; how exact they have to be, the bound alone decides.
A program may use at most 64 MiB of HBM per device.

v0:
```python
import math
import jax
import jax.numpy as jnp
from jax import lax
from jax.sharding import PartitionSpec as P

epsilon = 1e-05
highest = lax.Precision.HIGHEST
lowest_start = -1e30


def from_root(shard, axis, root):
    mine = lax.axis_index(axis) == root
    return lax.psum(jnp.where(mine, shard, jnp.zeros_like(shard)), axis)


def layer_normalise(values, norm_gain):
    average = jnp.mean(values, axis=-1, keepdims=True)
    centred = values - average
    variance = jnp.mean(centred * centred, axis=-1, keepdims=True)
    return centred * lax.rsqrt(variance + epsilon) * norm_gain


def apply_projection(values, weight):
    return jnp.einsum("...c,cd->...d", values, weight, precision=highest)


def transition_update(values, norm_gain, feedforward_expand_kernel, feedforward_shrink_kernel):
    expanded = jax.nn.relu(
        apply_projection(layer_normalise(values, norm_gain), feedforward_expand_kernel)
    )
    return values + apply_projection(expanded, feedforward_shrink_kernel)


def online_update(state_carry, scores, values, einsum_form):
    running_max, sum_weights, numerator = state_carry
    new_max = jnp.maximum(running_max, jnp.max(scores, axis=-1))
    weights = jnp.exp(scores - new_max[..., None])
    sum_weights = jnp.sum(weights, axis=-1)
    numerator = jnp.einsum(einsum_form, weights, values, precision=highest)
    return (new_max, sum_weights, numerator)


def empty_state(leading, head_size):
    return (
        jnp.full(leading, lowest_start, jnp.float32),
        jnp.zeros(leading, jnp.float32),
        jnp.zeros(leading + (head_size,), jnp.float32),
    )


def panels(first_local, second_local):
    groups = lax.axis_size("gi") // lax.axis_size(("branch", "gj"))
    col_index = lax.axis_index(("branch", "gj"))
    first_panel, second_panel = (
        lax.all_gather(first_local, ("branch", "gj"), axis=1, tiled=True),
        lax.all_gather(second_local, ("branch", "gj"), axis=1, tiled=True),
    )
    pieces = from_root(second_panel, "gi", col_index * groups + 0)
    return (first_panel, pieces)


def per_device(
    homolog_embedding,
    pair_input_tensor,
    layernorm_scales,
    pair_norm_gains,
    pair_bias_matrix,
    horizontal_qkvg_kernel,
    horizontal_final_kernel,
    vertical_qkvg_kernel,
    vertical_final_kernel,
    feedforward_expand_kernel,
    feedforward_shrink_kernel,
    dyadic_sides_kernel,
    outer_output_matrix,
    triangle_input_matrix,
    triangle_output_matrix,
):
    rows_per_device, residues_per_device, alignment_width = homolog_embedding.shape
    pair_cols, pair_width = (pair_input_tensor.shape[1], pair_input_tensor.shape[2])
    head_count = pair_bias_matrix.shape[1]
    inner_feature_width = horizontal_final_kernel.shape[0]
    head_size = inner_feature_width // head_count
    outer_width = dyadic_sides_kernel.shape[1] // 2
    bias_local = apply_projection(
        layer_normalise(pair_input_tensor, pair_norm_gains[0]), pair_bias_matrix
    ).reshape(residues_per_device, pair_cols * head_count)
    bias_rows = lax.all_gather(bias_local, ("branch", "gj"), axis=1, tiled=True).reshape(
        residues_per_device, -1, head_count
    )
    bias_heads = jnp.transpose(bias_rows, (2, 0, 1))
    alignment_normalised = layer_normalise(homolog_embedding, layernorm_scales[0])
    row_query_values = apply_projection(
        alignment_normalised, horizontal_qkvg_kernel[:, :inner_feature_width]
    ).reshape(rows_per_device, residues_per_device, head_count, head_size)
    row_gate_values = apply_projection(
        alignment_normalised, horizontal_qkvg_kernel[:, 3 * inner_feature_width :]
    )
    row_start = empty_state((rows_per_device, head_count, residues_per_device), head_size)
    row_pair_slice = apply_projection(
        alignment_normalised,
        horizontal_qkvg_kernel[:, inner_feature_width : 3 * inner_feature_width],
    )
    pieces = (
        lax.all_gather(row_pair_slice[..., :inner_feature_width], "gi", axis=1, tiled=True),
        lax.all_gather(row_pair_slice[..., inner_feature_width:], "gi", axis=1, tiled=True),
    )
    key_flat = pieces[0]
    block_rows = key_flat.shape[1]
    key_block = key_flat.reshape(rows_per_device, block_rows, head_count, head_size)
    value_block = pieces[1].reshape(rows_per_device, block_rows, head_count, head_size)
    scores = (
        jnp.einsum("sihd,sjhd->shij", row_query_values, key_block, precision=highest)
        / math.sqrt(head_size)
        + bias_heads[None]
    )
    row_state = online_update(row_start, scores, value_block, "shij,sjhd->shid")
    row_heads = row_state[2] / row_state[1][..., None]
    row_attention_result = jnp.transpose(row_heads, (0, 2, 1, 3)).reshape(
        rows_per_device, residues_per_device, inner_feature_width
    )
    alignment_after_rows = homolog_embedding + apply_projection(
        jax.nn.sigmoid(row_gate_values) * row_attention_result, horizontal_final_kernel
    )
    column_normalised = layer_normalise(alignment_after_rows, layernorm_scales[1])
    column_query = apply_projection(
        column_normalised, vertical_qkvg_kernel[:, :inner_feature_width]
    ).reshape(rows_per_device, residues_per_device, head_count, head_size)
    column_pairs = apply_projection(
        column_normalised, vertical_qkvg_kernel[:, inner_feature_width : 3 * inner_feature_width]
    )
    column_gate_values = apply_projection(
        column_normalised, vertical_qkvg_kernel[:, 3 * inner_feature_width :]
    )
    column_start = empty_state((residues_per_device, head_count, rows_per_device), head_size)
    pieces = (
        lax.all_gather(
            column_pairs[..., :inner_feature_width], ("branch", "gj"), axis=0, tiled=True
        ),
        lax.all_gather(
            column_pairs[..., inner_feature_width:], ("branch", "gj"), axis=0, tiled=True
        ),
    )
    block_rows = pieces[0].shape[0]
    key_block = pieces[0].reshape(block_rows, residues_per_device, head_count, head_size)
    value_block = pieces[1].reshape(block_rows, residues_per_device, head_count, head_size)
    scores = jnp.einsum("sihd,tihd->ihst", column_query, key_block, precision=highest) / math.sqrt(
        head_size
    )
    column_state = online_update(column_start, scores, value_block, "ihst,tihd->ihsd")
    column_heads = column_state[2] / column_state[1][..., None]
    column_attention_result = jnp.transpose(column_heads, (2, 0, 1, 3)).reshape(
        rows_per_device, residues_per_device, inner_feature_width
    )
    alignment_after_columns = alignment_after_rows + apply_projection(
        jax.nn.sigmoid(column_gate_values) * column_attention_result, vertical_final_kernel
    )
    alignment_output = transition_update(
        alignment_after_columns,
        layernorm_scales[2],
        feedforward_expand_kernel,
        feedforward_shrink_kernel,
    )
    factor_pair = apply_projection(
        layer_normalise(alignment_output, layernorm_scales[3]), dyadic_sides_kernel
    )
    left_local = jnp.transpose(factor_pair[..., :outer_width], (1, 0, 2)).reshape(
        residues_per_device, rows_per_device * outer_width
    )
    right_local = jnp.transpose(factor_pair[..., outer_width:], (1, 0, 2)).reshape(
        residues_per_device, rows_per_device * outer_width
    )
    left_panel, right_panel = panels(left_local, right_local)
    all_rows = left_panel.shape[1] // outer_width
    left_three = left_panel.reshape(residues_per_device, all_rows, outer_width)
    right_three = right_panel.reshape(pair_cols, all_rows, outer_width)
    outer = jnp.einsum("isc,jsd->ijcd", left_three, right_three, precision=highest) / all_rows
    pair_first = pair_input_tensor + apply_projection(
        outer.reshape(residues_per_device, pair_cols, outer_width * outer_width),
        outer_output_matrix,
    )
    projected_values = apply_projection(
        layer_normalise(pair_first, pair_norm_gains[1]), triangle_input_matrix
    )
    left_tri = (
        jax.nn.sigmoid(projected_values[..., pair_width : 2 * pair_width])
        * projected_values[..., :pair_width]
    )
    right_tri = (
        jax.nn.sigmoid(projected_values[..., 3 * pair_width : 4 * pair_width])
        * projected_values[..., 2 * pair_width : 3 * pair_width]
    )
    out_gate = projected_values[..., 4 * pair_width :]
    left_rows, right_rows = panels(
        left_tri.reshape(residues_per_device, pair_cols * pair_width),
        right_tri.reshape(residues_per_device, pair_cols * pair_width),
    )
    left_rows = left_rows.reshape(residues_per_device, -1, pair_width)
    right_rows = right_rows.reshape(pair_cols, -1, pair_width)
    product = jnp.einsum("ikc,jkc->ijc", left_rows, right_rows, precision=highest)
    pair_output_tensor = pair_first + jax.nn.sigmoid(out_gate) * apply_projection(
        layer_normalise(product, pair_norm_gains[2]), triangle_output_matrix
    )
    return (alignment_output, pair_output_tensor)


def solution(mesh):
    return jax.shard_map(
        per_device,
        mesh=mesh,
        in_specs=(
            P(("branch", "gj"), "gi", None),
            P("gi", ("branch", "gj"), None),
            P(),
            P(),
            P(),
            P(),
            P(),
            P(),
            P(),
            P(),
            P(),
            P(),
            P(),
            P(),
            P(),
        ),
        out_specs=(P(("branch", "gj"), "gi", None), P("gi", ("branch", "gj"), None)),
        check_vma=False,
    )
```

profile of v0, /device:TPU:2, one launch (start us, length us, event | category | flops | bytes accessed | tf_op | source)
XLA Modules:
  0.0 740.1 jit_solution(3773819482061920002)
XLA Ops:
  17.5 40.2 %all_gather.28 = f32[16,2048]{0,1:T(8,128)S(1)} all-gather(f32[16,128]{0,1:T(8,128)S(1)} %convolution_bitcast_fusion.2), channel_id=1, replica_groups=mesh['branch'=2,'gi'=16,'gj'=8] {'branch','gj'}, dimensions={1}, use_global_device_ids=true | all-gather | bytes 139264 | tf_op jit(solution)/shard_map/all_gather | solution.py:89
  58.1 44.4 %all-gather.7.cloned.1.call-done = f32[8,256,256]{2,1,0:T(8,128)} async-done(((f32[8,16,256]{2,1,0:T(8,128)}), f32[8,256,256]{2,1,0:T(8,128)}) %all-gather.7.cloned.1.call-update) | async-done | bytes 2097168 | tf_op jit(solution)/shard_map/all_gather | solution.py:106
  102.4 2.9 copy.90
  105.4 2.9 fusion.101
  108.7 79.0 %all-gather.9.cloned.1.call-done = f32[8,256,256]{2,1,0:T(8,128)} async-done(((f32[8,16,256]{2,1,0:T(8,128)}), f32[8,256,256]{2,1,0:T(8,128)}) %all-gather.9.cloned.1.call-update) | async-done | bytes 2097168 | tf_op jit(solution)/shard_map/all_gather | solution.py:107
  187.7 2.9 copy.94
  190.6 3.5 fusion.1
  200.7 30.8 %all-gather.11.cloned.1.call-done = f32[128,16,256]{2,1,0:T(8,128)} async-done(((f32[8,16,256]{2,1,0:T(8,128)}), f32[128,16,256]{2,1,0:T(8,128)}) %all-gather.11.cloned.1.call-update) | async-done | bytes 2097168 | tf_op jit(solution)/shard_map/all_gather | solution.py:138
  233.4 3.2 fusion.103
  237.8 32.4 %all-gather.13.cloned.1.call-done = f32[128,16,256]{2,1,0:T(8,128)} async-done(((f32[8,16,256]{2,1,0:T(8,128)}), f32[128,16,256]{2,1,0:T(8,128)}) %all-gather.13.cloned.1.call-update) | async-done | bytes 2097168 | tf_op jit(solution)/shard_map/all_gather | solution.py:141
  272.2 4.5 fusion.2
  281.4 28.4 %all_gather.32 = f32[16,4096]{1,0:T(8,128)S(1)} all-gather(f32[16,256]{1,0:T(8,128)S(1)} %reshape.171), channel_id=1, replica_groups=mesh['branch'=2,'gi'=16,'gj'=8] {'branch','gj'}, dimensions={1}, use_global_device_ids=true | all-gather | bytes 278528 | tf_op jit(solution)/shard_map/all_gather | solution.py:57
  311.3 28.2 %all_gather.33 = f32[16,4096]{1,0:T(8,128)S(1)} all-gather(f32[16,256]{1,0:T(8,128)S(1)} %reshape.173), channel_id=1, replica_groups=mesh['branch'=2,'gi'=16,'gj'=8] {'branch','gj'}, dimensions={1}, use_global_device_ids=true | all-gather | bytes 278528 | tf_op jit(solution)/shard_map/all_gather | solution.py:56
  339.8 128.2 %all-reduce.3.cloned.1.call-done = f32[16,128,32]{1,2,0:T(8,128)} async-done(((f32[16,128,32]{1,2,0:T(8,128)}), f32[16,128,32]{1,2,0:T(8,128)}) %all-reduce.3.cloned.1.call-update) | async-done | bytes 262160 | tf_op jit(solution)/shard_map/psum | solution.py:14
  468.1 5.9 multiply_bitcast_fusion
  473.9 5.4 copy.104
  479.3 3.8 reshape.175
  487.7 32.8 %all-gather.15.cloned.1.call-done = f32[16,32768]{1,0:T(8,128)} async-done(((f32[16,2048]{1,0:T(8,128)}), f32[16,32768]{1,0:T(8,128)}) %all-gather.15.cloned.1.call-update) | async-done | bytes 2097168 | tf_op jit(solution)/shard_map/all_gather | solution.py:57
  521.0 2.1 copy.105
  523.1 35.6 %all-gather.17.cloned.1.call-done = f32[16,32768]{1,0:T(8,128)} async-done(((f32[16,2048]{1,0:T(8,128)}), f32[16,32768]{1,0:T(8,128)}) %all-gather.17.cloned.1.call-update) | async-done | bytes 2097168 | tf_op jit(solution)/shard_map/all_gather | solution.py:56
  558.7 3.3 copy.122
  562.1 2.2 copy.106
  564.4 160.5 %all-reduce.5.cloned.1.call-done = f32[16,256,128]{1,0,2:T(8,128)} async-done(((f32[16,256,128]{1,0,2:T(8,128)}), f32[16,256,128]{1,0,2:T(8,128)}) %all-reduce.5.cloned.1.call-update) | async-done | bytes 2097168 | tf_op jit(solution)/shard_map/psum | solution.py:14
  724.8 4.6 bitcast_reduce_fusion
  (124 shorter events, 37.7 us)
Async XLA Ops:
  7.2 272.0 %copy-start = (f32[256,1024]{1,0:T(8,128)S(1)}, f32[256,1024]{1,0:T(8,128)}, u32[]{:S(2)}) copy-start(f32[256,1024]{1,0:T(8,128)} %param.24) | copy-start | bytes 3145732
  7.2 6.9 copy-start.2
  7.2 6.7 copy-start.4
  7.2 8.5 %copy-start.15 = (f32[3,128]{1,0:T(4,128)S(1)}, f32[3,128]{1,0:T(4,128)}, u32[]{:S(2)}) copy-start(f32[3,128]{1,0:T(4,128)} %param.18) | copy-start | bytes 4612
  7.2 9.3 %copy-start.13 = (f32[128,8]{0,1:T(8,128)S(1)}, f32[128,8]{0,1:T(8,128)}, u32[]{:S(2)}) copy-start(f32[128,8]{0,1:T(8,128)} %param.19) | copy-start | bytes 12292
  7.2 95.2 %all-gather.7.cloned.1.call-start = ((), (), s32[]{:S(2)}) async-start(), calls=%async_computation | async-start | bytes 2228224 | tf_op jit(solution)/shard_map/all_gather | solution.py:106
  13.1 174.6 %all-gather.9.cloned.1.call-start = ((), (), s32[]{:S(2)}) async-start(), calls=%async_computation.1 | async-start | bytes 2228224 | tf_op jit(solution)/shard_map/all_gather | solution.py:107
  13.9 217.6 %all-gather.11.cloned.1.call-start = ((), (), s32[]{:S(2)}) async-start(), calls=%async_computation.2 | async-start | bytes 2228224 | tf_op jit(solution)/shard_map/all_gather | solution.py:138
  194.2 3.2 copy-start.7
  198.6 71.6 %all-gather.13.cloned.1.call-start = ((), (), s32[]{:S(2)}) async-start(), calls=%async_computation.3 | async-start | bytes 2228224 | tf_op jit(solution)/shard_map/all_gather | solution.py:141
  199.2 268.9 %all-reduce.3.cloned.1.call-start = ((), (), s32[]{:S(2)}) async-start(), calls=%async_computation.4 | async-start | bytes 524288 | tf_op jit(solution)/shard_map/psum | solution.py:14
  276.6 1.9 copy-start.10
  276.6 2.5 copy-start.12
  276.8 3.1 copy-start.6
  278.9 1.9 copy-start.11
  280.6 30.5 %copy-start.5 = (f32[8,16,256]{2,1,0:T(8,128)}, f32[8,16,256]{2,1,0:T(8,128)S(1)}, u32[]{:S(2)}) copy-start(f32[8,16,256]{2,1,0:T(8,128)S(1)} %get-tuple-element.26) | copy-start | bytes 393220
  311.1 209.3 %all-gather.15.cloned.1.call-start = ((), (), s32[]{:S(2)}) async-start(), calls=%async_computation.5 | async-start | bytes 2228224 | tf_op jit(solution)/shard_map/all_gather | solution.py:57
  479.3 3.8 copy-start.8
  479.3 5.1 copy-start.14
  483.1 1.3 copy-start.9
  486.9 71.9 %all-gather.17.cloned.1.call-start = ((), (), s32[]{:S(2)}) async-start(), calls=%async_computation.7 | async-start | bytes 2228224 | tf_op jit(solution)/shard_map/all_gather | solution.py:56
  487.6 237.2 %all-reduce.5.cloned.1.call-start = ((), (), s32[]{:S(2)}) async-start(), calls=%async_computation.6 | async-start | bytes 4194304 | tf_op jit(solution)/shard_map/psum | solution.py:14
  564.3 167.1 %copy-start.16 = (f32[128]{0:T(128)S(1)}, f32[128]{0:T(128)}, u32[]{:S(2)}) copy-start(f32[128]{0:T(128)} %get-tuple-element.14) | copy-start | bytes 1540
  564.3 167.1 %copy-start.17 = (f32[128,128]{1,0:T(8,128)S(1)}, f32[128,128]{1,0:T(8,128)}, u32[]{:S(2)}) copy-start(f32[128,128]{1,0:T(8,128)} %param.29) | copy-start | bytes 196612
  (2 other events, 1.7 us)
Sparse Core Ops, SparseCore 0:
  13.3 89.1 all-gather.6
  105.6 82.0 all-gather.8
  198.7 32.7 all-gather.10
  233.7 36.3 all-gather.12
  311.2 156.7 all-reduce.2
  487.0 33.4 all-gather.14
  522.3 36.3 all-gather.16
  561.4 163.4 all-reduce.4
where the time goes:
time: 741 us; the launch traced here: 740 us
  waiting for transfers between devices  545 us (74%)
  blocking collectives  96.8 us (13%)
  local copies, waits for them, and re-layouts  39.3 us (5%)
  matrix products  39.2 us (5%)
  between operations  14.8 us (2%)
    psum x2, waiting for transfers between devices, from_root(): return lax.psum(jnp.where(mine, shard, jnp.zeros_like(shard)), axis)  289 us
    all_gather x1, waiting for transfers between devices, per_device(): lax.all_gather(row_pair_slice[..., inner_feature_width:], 'gi', axis=1, t...  79 us
    all_gather x1, waiting for transfers between devices, per_device(): lax.all_gather(row_pair_slice[..., :inner_feature_width], 'gi', axis=1, t...  44.4 us
    all_gather x1, blocking collectives, per_device(): lax.all_gather(bias_local, ('branch', 'gj'), axis=1, tiled=True)  40.2 us
    all_gather x1, waiting for transfers between devices, panels(): lax.all_gather(first_local, ('branch', 'gj'), axis=1, tiled=True)  35.6 us
    all_gather x1, waiting for transfers between devices, panels(): lax.all_gather(second_local, ('branch', 'gj'), axis=1, tiled=True)  32.8 us
    all_gather x1, waiting for transfers between devices, per_device(): lax.all_gather(column_pairs[..., inner_feature_width:], ('branch', 'gj'),...  32.4 us
    all_gather x1, waiting for transfers between devices, per_device(): lax.all_gather(column_pairs[..., :inner_feature_width], ('branch', 'gj'),...  30.8 us
  transfers between devices with their start and end apart: 8, of which 8 were waited for; matrix products, arithmetic and copies ran while one was open for 4% of the time, Pallas kernels for 0%

commit v1 on v0

--- a/solution.py
+++ b/solution.py
@@ -11,7 +11,7 @@
 
 def from_root(shard, axis, root):
     mine = lax.axis_index(axis) == root
-    return lax.psum(jnp.where(mine, shard, jnp.zeros_like(shard)), axis)
+    return jnp.sum(lax.all_gather(jnp.where(mine, shard, jnp.zeros_like(shard)), axis), axis=0)
 
 
 def layer_normalise(values, norm_gain):

time: 741 us -> 953 us (1.29)
  waiting for transfers between devices: 545 us -> 737 us
  other arithmetic: 4.57 us -> 22 us
    all_gather x0 -> x2, waiting for transfers between devices: none -> 481 us  [from_root(): lax.all_gather(jnp.where(mine, shard, jnp.zeros_like(shard)), axis)]
    psum x2 -> x0, waiting for transfers between devices: 289 us -> none  [from_root(): return lax.psum(jnp.where(mine, shard, jnp.zeros_like(shard)), axis)]
    reduce_sum x0 -> x2, other arithmetic: none -> 15.4 us  [from_root(): jnp.sum(lax.all_gather(jnp.where(mine, shard, jnp.zeros_like(shard)), axi...]
  transfers between devices with their start and end apart: 8 -> 8, of which waited for: 8 -> 8; matrix products, arithmetic and copies ran while one was open for 4% -> 3% of each run, Pallas kernels for 0% -> 0%
where the time goes in v1:
time: 953 us; the launch traced here: 952 us
  waiting for transfers between devices  737 us (77%)
  blocking collectives  97 us (10%)
  local copies, waits for them, and re-layouts  41.4 us (4%)
  matrix products  38.6 us (4%)
  other arithmetic  22 us (2%)
  between operations  14.8 us (2%)
    all_gather x2, waiting for transfers between devices, from_root(): lax.all_gather(jnp.where(mine, shard, jnp.zeros_like(shard)), axis)  481 us
    all_gather x1, waiting for transfers between devices, per_device(): lax.all_gather(row_pair_slice[..., inner_feature_width:], 'gi', axis=1, t...  79 us
    all_gather x1, waiting for transfers between devices, per_device(): lax.all_gather(row_pair_slice[..., :inner_feature_width], 'gi', axis=1, t...  44.3 us
    all_gather x1, blocking collectives, per_device(): lax.all_gather(bias_local, ('branch', 'gj'), axis=1, tiled=True)  40.3 us
    all_gather x1, waiting for transfers between devices, panels(): lax.all_gather(first_local, ('branch', 'gj'), axis=1, tiled=True)  36.8 us
    all_gather x1, waiting for transfers between devices, per_device(): lax.all_gather(column_pairs[..., inner_feature_width:], ('branch', 'gj'),...  32.4 us
    all_gather x1, waiting for transfers between devices, panels(): lax.all_gather(second_local, ('branch', 'gj'), axis=1, tiled=True)  31.9 us
    all_gather x1, waiting for transfers between devices, per_device(): lax.all_gather(column_pairs[..., :inner_feature_width], ('branch', 'gj'),...  30.8 us
  transfers between devices with their start and end apart: 8, of which 8 were waited for; matrix products, arithmetic and copies ran while one was open for 3% of the time, Pallas kernels for 0%

profile of v1, /device:TPU:2, one launch (start us, length us, event | category | flops | bytes accessed | tf_op | source)
XLA Modules:
  0.0 951.7 jit_solution(2299638661625144908)
XLA Ops:
  17.5 40.3 %all_gather.40 = f32[16,2048]{0,1:T(8,128)S(1)} all-gather(f32[16,128]{0,1:T(8,128)S(1)} %convolution_bitcast_fusion.2), channel_id=1, replica_groups=mesh['branch'=2,'gi'=16,'gj'=8] {'branch','gj'}, dimensions={1}, use_global_device_ids=true | all-gather | bytes 139264 | tf_op jit(solution)/shard_map/all_gather | solution.py:89
  58.2 44.3 %all-gather.11.cloned.1.call-done = f32[8,256,256]{2,1,0:T(8,128)} async-done(((f32[8,16,256]{2,1,0:T(8,128)}), f32[8,256,256]{2,1,0:T(8,128)}) %all-gather.11.cloned.1.call-update) | async-done | bytes 2097168 | tf_op jit(solution)/shard_map/all_gather | solution.py:106
  102.5 2.9 copy.90
  105.4 2.9 fusion.101
  108.7 79.0 %all-gather.13.cloned.1.call-done = f32[8,256,256]{2,1,0:T(8,128)} async-done(((f32[8,16,256]{2,1,0:T(8,128)}), f32[8,256,256]{2,1,0:T(8,128)}) %all-gather.13.cloned.1.call-update) | async-done | bytes 2097168 | tf_op jit(solution)/shard_map/all_gather | solution.py:107
  190.6 3.5 fusion.1
  200.7 30.8 %all-gather.15.cloned.1.call-done = f32[128,16,256]{2,1,0:T(8,128)} async-done(((f32[8,16,256]{2,1,0:T(8,128)}), f32[128,16,256]{2,1,0:T(8,128)}) %all-gather.15.cloned.1.call-update) | async-done | bytes 2097168 | tf_op jit(solution)/shard_map/all_gather | solution.py:138
  233.5 3.2 fusion.103
  237.8 32.4 %all-gather.17.cloned.1.call-done = f32[128,16,256]{2,1,0:T(8,128)} async-done(((f32[8,16,256]{2,1,0:T(8,128)}), f32[128,16,256]{2,1,0:T(8,128)}) %all-gather.17.cloned.1.call-update) | async-done | bytes 2097168 | tf_op jit(solution)/shard_map/all_gather | solution.py:141
  272.2 4.5 fusion.2
  281.4 28.4 %all_gather.44 = f32[16,4096]{1,0:T(8,128)S(1)} all-gather(f32[16,256]{1,0:T(8,128)S(1)} %reshape.171), channel_id=1, replica_groups=mesh['branch'=2,'gi'=16,'gj'=8] {'branch','gj'}, dimensions={1}, use_global_device_ids=true | all-gather | bytes 278528 | tf_op jit(solution)/shard_map/all_gather | solution.py:57
  310.6 28.3 %all_gather.47 = f32[16,4096]{1,0:T(8,128)S(1)} all-gather(f32[16,256]{1,0:T(8,128)S(1)} %reshape.173), channel_id=1, replica_groups=mesh['branch'=2,'gi'=16,'gj'=8] {'branch','gj'}, dimensions={1}, use_global_device_ids=true | all-gather | bytes 278528 | tf_op jit(solution)/shard_map/all_gather | solution.py:56
  339.3 70.8 %all-gather.23.cloned.1.call-done = f32[256,4096]{1,0:T(8,128)} async-done(((f32[16,4096]{1,0:T(8,128)}), f32[256,4096]{1,0:T(8,128)}) %all-gather.23.cloned.1.call-update) | async-done | bytes 4194320 | tf_op jit(solution)/shard_map/all_gather | solution.py:14
  412.9 5.2 multiply_bitcast_fusion
  418.1 5.4 copy.104
  423.4 3.8 reshape.175
  431.0 31.9 %all-gather.19.cloned.1.call-done = f32[16,32768]{1,0:T(8,128)} async-done(((f32[16,2048]{1,0:T(8,128)}), f32[16,32768]{1,0:T(8,128)}) %all-gather.19.cloned.1.call-update) | async-done | bytes 2097168 | tf_op jit(solution)/shard_map/all_gather | solution.py:57
  464.4 36.8 %all-gather.21.cloned.1.call-done = f32[16,32768]{1,0:T(8,128)} async-done(((f32[16,2048]{1,0:T(8,128)}), f32[16,32768]{1,0:T(8,128)}) %all-gather.21.cloned.1.call-update) | async-done | bytes 2097168 | tf_op jit(solution)/shard_map/all_gather | solution.py:56
  501.2 3.3 copy.124
  506.8 410.0 %all-gather.25.cloned.1.call-done = f32[256,32768]{1,0:T(8,128)} async-done(((f32[16,32768]{1,0:T(8,128)}), f32[256,32768]{1,0:T(8,128)}) %all-gather.25.cloned.1.call-update) | async-done | bytes 33554448 | tf_op jit(solution)/shard_map/all_gather | solution.py:14
  916.8 13.0 %reduce_sum.177 = f32[16,32768]{1,0:T(8,128)} reduce(f32[16,16,32768]{2,1,0:T(8,128)} %bitcast.135, f32[]{:T(128)} %constant.46.clone.1), dimensions={0}, to_apply=%region_17.18 | reduce | flops 7864320 | bytes 35651588 | tf_op jit(solution)/shard_map/reduce_sum | solution.py:14
  929.8 3.3 copy.122
  933.2 3.1 copy.105
  936.3 4.7 bitcast_reduce_fusion
  (127 shorter events, 45.0 us)
Async XLA Ops:
  7.2 272.0 %copy-start = (f32[256,1024]{1,0:T(8,128)S(1)}, f32[256,1024]{1,0:T(8,128)}, u32[]{:S(2)}) copy-start(f32[256,1024]{1,0:T(8,128)} %param.24) | copy-start | bytes 3145732
  7.2 6.9 copy-start.3
  7.2 6.7 copy-start.5
  7.2 8.5 copy-start.16
  7.2 9.3 copy-start.14
  7.2 95.2 %all-gather.11.cloned.1.call-start = ((), (), s32[]{:S(2)}) async-start(), calls=%async_computation | async-start | bytes 2228224 | tf_op jit(solution)/shard_map/all_gather | solution.py:106
  13.1 174.6 %all-gather.13.cloned.1.call-start = ((), (), s32[]{:S(2)}) async-start(), calls=%async_computation.1 | async-start | bytes 2228224 | tf_op jit(solution)/shard_map/all_gather | solution.py:107
  13.9 217.6 %all-gather.15.cloned.1.call-start = ((), (), s32[]{:S(2)}) async-start(), calls=%async_computation.2 | async-start | bytes 2228224 | tf_op jit(solution)/shard_map/all_gather | solution.py:138
  194.2 3.2 copy-start.8
  198.6 71.6 %all-gather.17.cloned.1.call-start = ((), (), s32[]{:S(2)}) async-start(), calls=%async_computation.3 | async-start | bytes 2228224 | tf_op jit(solution)/shard_map/all_gather | solution.py:141
  199.2 210.9 %all-gather.23.cloned.1.call-start = ((), (), s32[]{:S(2)}) async-start(), calls=%async_computation.6 | async-start | bytes 4456448 | tf_op jit(solution)/shard_map/all_gather | solution.py:14
  276.6 1.9 copy-start.11
  276.7 2.5 copy-start.13
  276.8 3.1 copy-start.7
  280.6 131.9 %copy-start.6 = (f32[8,16,256]{2,1,0:T(8,128)}, f32[8,16,256]{2,1,0:T(8,128)S(1)}, u32[]{:S(2)}) copy-start(f32[8,16,256]{2,1,0:T(8,128)S(1)} %get-tuple-element.26) | copy-start | bytes 393220
  310.5 152.5 %all-gather.19.cloned.1.call-start = ((), (), s32[]{:S(2)}) async-start(), calls=%async_computation.4 | async-start | bytes 2228224 | tf_op jit(solution)/shard_map/all_gather | solution.py:57
  423.4 3.8 copy-start.9
  423.4 5.1 copy-start.15
  429.3 35.1 %copy-start.4 = (f32[16,16,640]{2,1,0:T(8,128)}, f32[16,16,640]{2,1,0:T(8,128)S(1)}, u32[]{:S(2)}) copy-start(f32[16,16,640]{2,1,0:T(8,128)S(1)} %fusion.28) | copy-start | bytes 1966084
  430.2 71.0 %all-gather.21.cloned.1.call-start = ((), (), s32[]{:S(2)}) async-start(), calls=%async_computation.5 | async-start | bytes 2228224 | tf_op jit(solution)/shard_map/all_gather | solution.py:56
  431.0 485.8 %all-gather.25.cloned.1.call-start = ((), (), s32[]{:S(2)}) async-start(), calls=%async_computation.7 | async-start | bytes 35651584 | tf_op jit(solution)/shard_map/all_gather | solution.py:14
  936.3 6.7 copy-start.17
  936.3 6.7 copy-start.18
  936.3 8.6 copy-start.1
  (3 other events, 4.0 us)
Sparse Core Ops, SparseCore 0:
  13.3 89.1 all-gather.10
  105.6 82.0 all-gather.12
  198.7 32.7 all-gather.14
  233.7 36.3 all-gather.16
  310.6 99.4 all-gather.22
  430.3 32.5 all-gather.18
  464.8 36.3 all-gather.20
  503.8 412.9 all-gather.24
